TPU v7x, 256 devices: a whole 4x4x8 slice. The times are simulated.
256 devices in a mesh: owner: 64 (over z, x, core), col: 4 (over y).
Axes of the slice: x: 4, y: 4, z: 8, core: 2. Of those that a mesh axis runs over, the one named last changes fastest.
Arguments:
- momentum: float32 [128, 512, 2048], P(None, 'owner', 'col'), may hold values from -7200 to 7200
- hidden_acts: bfloat16 [32768, 512], P('owner'), may hold values from -6 to 6
- output_grads: bfloat16 [32768, 2048], P('owner', 'col'), may hold values from -6 to 6
- routing: int32 [32768], P('owner'), may hold values from 0 to 1
- assignment: int32 [128], replicated, may hold values from 0 to 127, each once
Outputs:
- new_momentum: float32 [128, 512, 2048], P(None, 'owner', 'col')
- update: float32 [128, 512, 2048], P('owner', None, 'col')
Inputs may be any that keep to these rules, and one draw needn't show every extreme that they name: `routing`: the row's expert as a local slot of the owner group that holds the row. `assignment`: a permutation: each expert is held in exactly one slot.
All inputs are finite; a program needn't handle non-finite values.
Results may differ from a plain program's by a relative error of at most 0.0065.
Values may be sent and summed in bfloat16 or wider, within the bound.
A program may use at most 64 MiB of HBM per device.

v0:
```python
import jax
import jax.numpy as jnp
from jax import lax
from jax.sharding import Mesh
from jax.sharding import PartitionSpec as P

D = 2048
FFE = 512
EXP_DEV = 2
NS_ITERS = 2
OWNER = ("owner_0", "owner_1", "owner_2")
decay_rate = 0.95
epsilon = 1e-07
linear_weight = 3.4445
cubic_weight = -4.775
quintic_weight = 2.0315


def from_everyone(array, axis):
    copies = jnp.broadcast_to(array, (lax.axis_size(axis), *array.shape))
    return lax.all_to_all(copies, axis, split_axis=0, concat_axis=0, tiled=True)


def taken_together(array, axis):
    return from_everyone(array, axis).sum(axis=0)


def split_up(array, dim, size):
    shape = array.shape
    parts = array.reshape(*shape[:dim], size, shape[dim] // size, *shape[dim + 1 :])
    return jnp.moveaxis(parts, dim, 0)


def laid_out(parts, dim):
    shape = list(parts.shape[1:])
    shape[dim] *= parts.shape[0]
    return jnp.moveaxis(parts, 0, dim).reshape(shape)


def turned_blocks(parts, axes, sequence):
    shape = [lax.axis_size(a) for a in axes]
    parts = parts.reshape(*shape, *parts.shape[1:])
    for k in sequence:
        parts = lax.all_to_all(parts, axes[k], split_axis=k, concat_axis=k, tiled=True)
    return parts.reshape(-1, *parts.shape[len(axes) :])


def core_and_chips(array, groups, sequence, split_dim, concat_dim):
    size = lax.axis_size(groups[0]) * lax.axis_size(groups[1])
    parts = split_up(array, split_dim, size)
    return laid_out(turned_blocks(parts, groups, sequence), concat_dim)


def newton_turn(iterate, gram_matrix):
    square = jnp.einsum(
        "jfg,jgh->jfh", gram_matrix, gram_matrix, preferred_element_type=jnp.float32
    )
    polynomial = (cubic_weight * gram_matrix.astype(jnp.float32) + quintic_weight * square).astype(
        jnp.bfloat16
    )
    product = jnp.einsum("jfg,jgd->jfd", polynomial, iterate, preferred_element_type=jnp.float32)
    return (linear_weight * iterate.astype(jnp.float32) + product).astype(jnp.bfloat16)


def body(momentum, hidden_acts, output_grads, routing, assignment):
    scaling = 0.2 * float(max(FFE, D)) ** 0.5
    columns = output_grads.shape[1]
    ordered = jnp.take(momentum, assignment, axis=0)
    received = lax.all_to_all(ordered, OWNER, split_axis=0, concat_axis=1, tiled=True)
    slot_ids = jnp.arange(EXP_DEV, dtype=jnp.int32)
    selected = routing[:, None, None] == slot_ids[None, :, None]
    masked = jnp.where(selected, output_grads[:, None, :], jnp.zeros((), jnp.bfloat16))
    gradient = jnp.einsum("rf,rjd->jfd", hidden_acts, masked, preferred_element_type=jnp.float32)
    updated = decay_rate * received + gradient
    squares = taken_together(jnp.sum(updated * updated, axis=(1, 2)), "col")
    iterate = (updated / (jnp.sqrt(squares)[:, None, None] + epsilon)).astype(jnp.bfloat16)
    complete = lax.all_gather(iterate, "col", axis=2, tiled=True)
    for turn_index in range(NS_ITERS):
        gram_matrix = jnp.einsum(
            "jfd,jgd->jfg", complete, complete, preferred_element_type=jnp.float32
        ).astype(jnp.bfloat16)
        complete = newton_turn(complete, gram_matrix)
    result_cols = lax.dynamic_slice_in_dim(complete, lax.axis_index("col") * columns, columns, 2)
    update = scaling * result_cols.astype(jnp.float32)
    returned = core_and_chips(
        updated.astype(jnp.bfloat16), (("owner_0", "owner_1"), "owner_2"), (1, 0), 1, 0
    ).astype(updated.dtype)
    new_momentum = jnp.zeros_like(momentum).at[assignment].set(returned)
    return (new_momentum, update)


def solution(mesh):
    torus = Mesh(
        mesh.devices.reshape(8, 4, 2, mesh.shape["col"]), ("owner_0", "owner_1", "owner_2", "col")
    )
    return jax.shard_map(
        body,
        mesh=torus,
        in_specs=(P(None, OWNER, "col"), P(OWNER, None), P(OWNER, "col"), P(OWNER), P()),
        out_specs=(P(None, OWNER, "col"), P(OWNER, None, "col")),
        check_vma=False,
    )
```

profile of v0, /device:TPU:2, one launch (start us, length us, event | category | flops | bytes accessed | tf_op | source)
XLA Modules:
  0.0 192.8 jit_solution(2016149358250970594)
XLA Ops:
  7.2 0.0 copy-start
  7.2 0.8 compare_select_fusion
  8.0 0.7 compare_and_fusion
  8.7 0.1 copy-done
  8.8 2.1 %gather_fusion = f32[128,8,512]{2,1,0:T(8,128)} fusion(f32[128,8,512]{2,1,0:T(8,128)S(1)} %copy-done, s32[1024]{0:T(1024)S(1)} %pad_clamp_fusion), kind=kCustom, calls=%fused_computation | custom fusion | bytes 4194816 | tf_op jit(solution)/shard_map/jit(_take)/gather | solution.py:68
  10.9 3.1 %broadcast_select_fusion = f32[128,8,512]{2,1,0:T(8,128)} fusion(f32[128,8,512]{2,1,0:T(8,128)} %gather_fusion, pred[128]{0:T(512)(128)(4,1)S(1)} %compare_and_fusion), kind=kLoop, calls=%fused_computation.16 | loop fusion | flops 524288 | bytes 4194432 | tf_op jit(solution)/shard_map/jit(_take)/select_n | solution.py:68
  14.0 0.0 copy-start.1
  14.0 12.3 %all-to-all-start = ((f32[128,8,512]{2,1,0:T(8,128)}), f32[128,8,512]{2,1,0:T(8,128)}, u32[]{:S(2)}, u32[]{:S(2)}) async-start(f32[128,8,512]{2,1,0:T(8,128)} %broadcast_select_fusion), calls=%async_computation | async-start | bytes 4194304 | tf_op jit(solution)/shard_map/all_to_all | solution.py:69
  26.4 0.0 all-gather.2.cloned.1.call-start
  26.4 0.0 copy-done.1
  26.4 0.0 copy-start.2
  26.4 51.1 %all-to-all-done = f32[128,8,512]{2,1,0:T(8,128)} async-done(((f32[128,8,512]{2,1,0:T(8,128)}), f32[128,8,512]{2,1,0:T(8,128)}, u32[]{:S(2)}, u32[]{:S(2)}) %all-to-all-start) | async-done | bytes 2097184 | tf_op jit(solution)/shard_map/all_to_all | solution.py:69
  77.5 0.0 copy-start.3
  77.5 1.9 broadcast_multiply_fusion
  79.4 0.0 copy-done.2
  79.4 0.0 copy-done.3
  79.4 2.2 %multiply_reduce_fusion = (f32[2]{0:T(128)S(1)}, f32[2,512,512]{2,1,0:T(8,128)}) fusion(bf16[512,512]{1,0:T(8,128)(2,1)S(1)} %copy-done.2, pred[512,2]{0,1:T(4,128)(4,1)S(1)} %iota_compare_fusion, bf16[512,512]{1,0:T(8,128)(2,1)S(1)} %copy-done.3, f32[64,2,8,512]{3,2,1,0:T(8,128)S(1)} %bitcast.31), kind=kOutput, calls=%fused_computation.10 | convolution fusion | flops 538968064 | bytes 5243912 | tf_op jit(solution)/shard_map/rf,rjd->jfd/dot_general | solution.py:73
  81.7 9.5 %all_to_all.25 = f32[4,1,2]{2,1,0:T(1,128)S(1)} all-to-all(f32[4,1,2]{2,1,0:T(1,128)S(1)} %broadcast_in_dim.50), channel_id=1, replica_groups=mesh['owner_0'=8,'owner_1'=4,'owner_2'=2,'col'=4] {'col'}, dimensions={0} | all-to-all | bytes 64 | tf_op jit(solution)/shard_map/all_to_all | solution.py:21
  91.2 3.6 %divide_convert_fusion = (bf16[2,512,512]{2,1,0:T(8,128)(2,1)}, bf16[2,512,512]{2,1,0:T(8,128)(2,1)S(1)}) fusion(f32[2,512,512]{2,1,0:T(8,128)} %get-tuple-element.5, f32[2]{0:T(128)S(1)} %sqrt_add_fusion), kind=kLoop, calls=%fused_computation.9 | loop fusion | flops 1572864 | bytes 4194312 | tf_op jit(solution)/shard_map/convert_element_type | solution.py:76
  94.9 0.0 all-gather.2.cloned.1.call-update
  94.9 0.2 copy.28
  95.1 4.6 %all_to_all.26 = bf16[32,2,2,8,512]{4,3,2,0,1:T(8,128)(2,1)S(1)} all-to-all(bf16[32,2,2,8,512]{4,3,2,0,1:T(8,128)(2,1)S(1)} %copy.28), channel_id=1, replica_groups=mesh['owner_0'=8,'owner_1'=4,'owner_2'=2,'col'=4] {'owner_2'}, dimensions={1} | all-to-all | bytes 2097152 | tf_op jit(solution)/shard_map/all_to_all | solution.py:44
  99.6 1.1 copy.29
  100.7 5.0 %all-to-all-start.2 = ((bf16[32,2,2,8,512]{4,3,2,1,0:T(8,128)(2,1)}), bf16[32,2,2,8,512]{4,3,2,1,0:T(8,128)(2,1)S(1)}, u32[]{:S(2)}, u32[]{:S(2)}) async-start(bf16[32,2,2,8,512]{4,3,2,1,0:T(8,128)(2,1)} %copy.29), calls=%async_computation.2 | async-start | bytes 2097152 | tf_op jit(solution)/shard_map/all_to_all | solution.py:44
  105.8 28.4 %all-to-all-done.2 = bf16[32,2,2,8,512]{4,3,2,1,0:T(8,128)(2,1)S(1)} async-done(((bf16[32,2,2,8,512]{4,3,2,1,0:T(8,128)(2,1)}), bf16[32,2,2,8,512]{4,3,2,1,0:T(8,128)(2,1)S(1)}, u32[]{:S(2)}, u32[]{:S(2)}) %all-to-all-start.2) | async-done | bytes 1048608 | tf_op jit(solution)/shard_map/all_to_all | solution.py:44
  134.1 1.7 bitcast_convert_fusion
  135.8 1.6 broadcast_in_dim.43
  137.4 17.6 %scatter_fusion = f32[128,8,512]{2,1,0:T(8,128)} fusion(f32[128,8,512]{2,1,0:T(8,128)} %broadcast_in_dim.43, s32[128]{0:T(128)S(1)} %compare_select_fusion, f32[128,8,512]{2,1,0:T(8,128)} %bitcast_convert_fusion), kind=kCustom, calls=%fused_computation.1 | custom fusion | bytes 6291968 | tf_op jit(solution)/shard_map/scatter | solution.py:88
  155.0 0.0 all-gather.2.cloned.1.call-done
  155.0 5.8 %convolution_convert_fusion.1 = bf16[2,512,512]{2,1,0:T(8,128)(2,1)S(1)} fusion(bf16[2,512,2048]{2,1,0:T(8,128)(2,1)} %all-gather.2.cloned.1.call-done), kind=kOutput, calls=%fused_computation.12 | convolution fusion | flops 2148007936 | bytes 5242880 | tf_op jit(solution)/shard_map/jfd,jgd->jfg/dot_general | solution.py:79
  160.9 7.4 %add_convert_fusion = bf16[2,512,2048]{2,1,0:T(8,128)(2,1)} fusion(bf16[2,512,2048]{2,1,0:T(8,128)(2,1)} %all-gather.2.cloned.1.call-done, bf16[2,512,512]{2,1,0:T(8,128)(2,1)S(1)} %convolution_convert_fusion.1), kind=kOutput, calls=%fused_computation.2 | convolution fusion | flops 2695364608 | bytes 9437184 | tf_op jit(solution)/shard_map/jfg,jgd->jfd/dot_general | solution.py:61
  168.2 5.8 %convolution_convert_fusion = bf16[2,512,512]{2,1,0:T(8,128)(2,1)S(1)} fusion(bf16[2,512,2048]{2,1,0:T(8,128)(2,1)} %add_convert_fusion), kind=kOutput, calls=%fused_computation.11 | convolution fusion | flops 2148007936 | bytes 5242880 | tf_op jit(solution)/shard_map/jfd,jgd->jfg/dot_general | solution.py:79
  174.0 8.3 %fusion.3 = f32[2,512,2048]{2,1,0:T(8,128)} fusion(bf16[2,512,2048]{2,1,0:T(8,128)(2,1)} %add_convert_fusion, bf16[2,512,512]{2,1,0:T(8,128)(2,1)S(1)} %convolution_convert_fusion), kind=kOutput, calls=%fused_computation.18 | convolution fusion | flops 2686976000 | bytes 13631488 | tf_op jit(solution)/shard_map/jfg,jgd->jfd/dot_general | solution.py:61
  182.4 3.6 %convert_multiply_fusion = f32[2,512,512]{2,1,0:T(8,128)} fusion(f32[2,512,2048]{2,1,0:T(8,128)} %fusion.3, s32[]{:T(128)S(6)} %select_n.20, bf16[2,512,2048]{2,1,0:T(8,128)(2,1)} %add_convert_fusion), kind=kLoop, calls=%fused_computation.6 | loop fusion | flops 3145728 | bytes 5242884 | tf_op jit(solution)/shard_map/mul | solution.py:84
  (5 shorter events, 0.1 us)
Async XLA Ops:
  7.2 1.6 copy-start
  14.0 12.4 %copy-start.1 = (s32[512]{0:T(512)S(1)}, s32[512]{0:T(512)}, u32[]{:S(2)}) copy-start(s32[512]{0:T(512)} %param.8) | copy-start | bytes 6148
  14.0 63.5 %all-to-all-start = ((f32[128,8,512]{2,1,0:T(8,128)}), f32[128,8,512]{2,1,0:T(8,128)}, u32[]{:S(2)}, u32[]{:S(2)}) async-start(f32[128,8,512]{2,1,0:T(8,128)} %broadcast_select_fusion), calls=%async_computation | async-start | bytes 4194304 | tf_op jit(solution)/shard_map/all_to_all | solution.py:69
  26.4 128.7 %all-gather.2.cloned.1.call-start = ((), (), s32[]{:S(2)}) async-start(), calls=%async_computation.4 | async-start | bytes 5242880 | tf_op jit(solution)/shard_map/all_gather | solution.py:77
  26.4 53.0 %copy-start.2 = (bf16[512,512]{1,0:T(8,128)(2,1)S(1)}, bf16[512,512]{1,0:T(8,128)(2,1)}, u32[]{:S(2)}) copy-start(bf16[512,512]{1,0:T(8,128)(2,1)} %param.6) | copy-start | bytes 1572868
  77.5 1.9 copy-start.3
  100.7 33.4 %all-to-all-start.2 = ((bf16[32,2,2,8,512]{4,3,2,1,0:T(8,128)(2,1)}), bf16[32,2,2,8,512]{4,3,2,1,0:T(8,128)(2,1)S(1)}, u32[]{:S(2)}, u32[]{:S(2)}) async-start(bf16[32,2,2,8,512]{4,3,2,1,0:T(8,128)(2,1)} %copy.29), calls=%async_computation.2 | async-start | bytes 2097152 | tf_op jit(solution)/shard_map/all_to_all | solution.py:44
Sparse Core Ops, SparseCore 0:
  95.0 45.1 all-gather.1
where the time goes:
time: 193 us
  waiting for transfers between devices  79.4 us (41%)
  matrix products  29.6 us (15%)
  local copies, waits for them, and re-layouts  22.7 us (12%)
  starting transfers between devices  17.4 us (9%)
  other arithmetic  15.4 us (8%)
  blocking collectives  14.1 us (7%)
  between operations  14.1 us (7%)
    all_to_all x1, waiting for transfers between devices, body(): lax.all_to_all(ordered, OWNER, split_axis=0, concat_axis=1, tiled=True)  51.1 us
    all_to_all x1, waiting for transfers between devices, turned_blocks(): lax.all_to_all(parts, axes[k], split_axis=k, concat_axis=k, tiled=True)  28.4 us
    scatter x1, local copies, waits for them, and re-layouts, body(): new_momentum = jnp.zeros_like(momentum).at[assignment].set(returned)  17.6 us
    dot_general x2, matrix products, newton_turn(): jnp.einsum('jfg,jgd->jfd', polynomial, iterate, preferred_element_type=jn...  15.7 us
    all_to_all x1, starting transfers between devices, body(): lax.all_to_all(ordered, OWNER, split_axis=0, concat_axis=1, tiled=True)  12.3 us
    dot_general x2, matrix products, body(): jnp.einsum('jfd,jgd->jfg', complete, complete, preferred_element_type=jnp...  11.6 us
    all_to_all x1, blocking collectives, from_everyone(): return lax.all_to_all(copies, axis, split_axis=0, concat_axis=0, tiled=True)  9.54 us
    all_to_all x1, starting transfers between devices, turned_blocks(): lax.all_to_all(parts, axes[k], split_axis=k, concat_axis=k, tiled=True)  5.04 us
  transfers between devices with their start and end apart: 3, of which 2 were waited for; matrix products, arithmetic and copies ran while one was open for 11% of the time, Pallas kernels for 0%

commit v1 on v0

--- a/solution.py
+++ b/solution.py
@@ -66,7 +66,10 @@
     scaling = 0.2 * float(max(FFE, D)) ** 0.5
     columns = output_grads.shape[1]
     ordered = jnp.take(momentum, assignment, axis=0)
-    received = lax.all_to_all(ordered, OWNER, split_axis=0, concat_axis=1, tiled=True)
+    received = jnp.concatenate(
+        lax.all_to_all(jnp.stack(jnp.split(ordered, lax.axis_size(OWNER), axis=0)), OWNER, 0, 0),
+        axis=1,
+    )
     slot_ids = jnp.arange(EXP_DEV, dtype=jnp.int32)
     selected = routing[:, None, None] == slot_ids[None, :, None]
     masked = jnp.where(selected, output_grads[:, None, :], jnp.zeros((), jnp.bfloat16))

time: 193 us -> 231 us (1.20)
  local copies, waits for them, and re-layouts: 22.7 us -> 62.2 us
  other arithmetic: 15.4 us -> 12.2 us
    unnamed x8 -> x69, local copies, waits for them, and re-layouts: 0.14 us -> 39 us
  transfers between devices with their start and end apart: 3 -> 3, of which waited for: 2 -> 2; matrix products, arithmetic and copies ran while one was open for 11% -> 10% of each run, Pallas kernels for 0% -> 0%
where the time goes in v1:
time: 231 us
  waiting for transfers between devices  79.5 us (34%)
  local copies, waits for them, and re-layouts  62.2 us (27%)
  matrix products  31.3 us (14%)
  starting transfers between devices  17.4 us (8%)
  blocking collectives  14.1 us (6%)
  between operations  14.1 us (6%)
  other arithmetic  12.2 us (5%)
    all_to_all x1, waiting for transfers between devices, body(): lax.all_to_all(jnp.stack(jnp.split(ordered, lax.axis_size(OWNER), axis=0)...  51.1 us
    unnamed x69, local copies, waits for them, and re-layouts  39 us
    all_to_all x1, waiting for transfers between devices, turned_blocks(): lax.all_to_all(parts, axes[k], split_axis=k, concat_axis=k, tiled=True)  28.4 us
    scatter x1, local copies, waits for them, and re-layouts, body(): new_momentum = jnp.zeros_like(momentum).at[assignment].set(returned)  17.6 us
    dot_general x2, matrix products, newton_turn(): jnp.einsum('jfg,jgd->jfd', polynomial, iterate, preferred_element_type=jn...  15.7 us
    all_to_all x1, starting transfers between devices, body(): lax.all_to_all(jnp.stack(jnp.split(ordered, lax.axis_size(OWNER), axis=0)...  12.3 us
    dot_general x2, matrix products, body(): jnp.einsum('jfd,jgd->jfg', complete, complete, preferred_element_type=jnp...  11.6 us
    all_to_all x1, blocking collectives, from_everyone(): return lax.all_to_all(copies, axis, split_axis=0, concat_axis=0, tiled=True)  9.54 us
  transfers between devices with their start and end apart: 3, of which 2 were waited for; matrix products, arithmetic and copies ran while one was open for 10% of the time, Pallas kernels for 0%

profile of v1, /device:TPU:2, one launch (start us, length us, event | category | flops | bytes accessed | tf_op | source)
XLA Modules:
  0.0 230.8 jit_solution(6788831557335494142)
XLA Ops:
  7.2 0.8 compare_select_fusion
  8.0 0.7 compare_and_fusion
  8.8 2.1 gather_fusion
  10.9 1.8 broadcast_select_fusion
  12.7 0.6 constant_dynamic-update-slice_fusion.63
  13.3 0.6 constant_dynamic-update-slice_fusion.62
  13.9 0.6 constant_dynamic-update-slice_fusion.61
  14.5 0.6 constant_dynamic-update-slice_fusion.60
  15.2 0.6 constant_dynamic-update-slice_fusion.59
  15.8 0.6 constant_dynamic-update-slice_fusion.58
  16.4 0.6 constant_dynamic-update-slice_fusion.57
  17.0 0.6 constant_dynamic-update-slice_fusion.56
  17.6 0.6 constant_dynamic-update-slice_fusion.55
  18.3 0.6 constant_dynamic-update-slice_fusion.54
  18.9 0.6 constant_dynamic-update-slice_fusion.53
  19.5 0.6 constant_dynamic-update-slice_fusion.52
  20.1 0.6 constant_dynamic-update-slice_fusion.51
  20.7 0.6 constant_dynamic-update-slice_fusion.50
  21.3 0.6 constant_dynamic-update-slice_fusion.49
  22.0 0.6 constant_dynamic-update-slice_fusion.48
  22.6 0.6 constant_dynamic-update-slice_fusion.47
  23.2 0.6 constant_dynamic-update-slice_fusion.46
  23.8 0.6 constant_dynamic-update-slice_fusion.45
  24.4 0.6 constant_dynamic-update-slice_fusion.44
  25.0 0.6 constant_dynamic-update-slice_fusion.43
  25.7 0.6 constant_dynamic-update-slice_fusion.42
  26.3 0.6 constant_dynamic-update-slice_fusion.41
  33.1 0.6 constant_dynamic-update-slice_fusion.30
  37.4 0.6 constant_dynamic-update-slice_fusion.23
  44.8 0.6 constant_dynamic-update-slice_fusion.11
  49.1 0.6 constant_dynamic-update-slice_fusion.4
  52.2 12.3 %all-to-all-start = ((f32[64,2,8,512]{3,2,1,0:T(8,128)}), f32[64,2,8,512]{3,2,1,0:T(8,128)}, u32[]{:S(2)}, u32[]{:S(2)}) async-start(f32[64,2,8,512]{3,2,1,0:T(8,128)} %constant_dynamic-update-slice_fusion), calls=%async_computation | async-start | bytes 4194304 | tf_op jit(solution)/shard_map/all_to_all | solution.py:70
  64.6 51.1 %all-to-all-done = f32[64,2,8,512]{3,2,1,0:T(8,128)} async-done(((f32[64,2,8,512]{3,2,1,0:T(8,128)}), f32[64,2,8,512]{3,2,1,0:T(8,128)}, u32[]{:S(2)}, u32[]{:S(2)}) %all-to-all-start) | async-done | bytes 2097184 | tf_op jit(solution)/shard_map/all_to_all | solution.py:70
  115.7 3.9 %multiply_reduce_fusion = (f32[2]{0:T(128)S(1)}, f32[2,512,512]{2,1,0:T(8,128)}) fusion(bf16[512,512]{1,0:T(8,128)(2,1)S(1)} %copy-done.2, pred[512,2]{0,1:T(4,128)(4,1)S(1)} %iota_compare_fusion, bf16[512,512]{1,0:T(8,128)(2,1)} %param.7, f32[64,2,8,512]{3,2,1,0:T(8,128)} %all-to-all-done), kind=kOutput, calls=%fused_computation.10 | convolution fusion | flops 539492352 | bytes 5243912 | tf_op jit(solution)/shard_map/rf,rjd->jfd/dot_general | solution.py:76
  119.7 9.5 %all_to_all.21 = f32[4,1,2]{2,1,0:T(1,128)S(1)} all-to-all(f32[4,1,2]{2,1,0:T(1,128)S(1)} %broadcast_in_dim.50), channel_id=1, replica_groups=mesh['owner_0'=8,'owner_1'=4,'owner_2'=2,'col'=4] {'col'}, dimensions={0} | all-to-all | bytes 64 | tf_op jit(solution)/shard_map/all_to_all | solution.py:21
  129.2 3.6 %divide_convert_fusion = (bf16[2,512,512]{2,1,0:T(8,128)(2,1)}, bf16[2,512,512]{2,1,0:T(8,128)(2,1)S(1)}) fusion(f32[2,512,512]{2,1,0:T(8,128)} %get-tuple-element.5, f32[2]{0:T(128)S(1)} %sqrt_add_fusion), kind=kLoop, calls=%fused_computation.9 | loop fusion | flops 1572864 | bytes 4194312 | tf_op jit(solution)/shard_map/convert_element_type | solution.py:79
  133.1 4.6 %all_to_all.22 = bf16[32,2,2,8,512]{4,3,2,0,1:T(8,128)(2,1)S(1)} all-to-all(bf16[32,2,2,8,512]{4,3,2,0,1:T(8,128)(2,1)S(1)} %copy.28), channel_id=1, replica_groups=mesh['owner_0'=8,'owner_1'=4,'owner_2'=2,'col'=4] {'owner_2'}, dimensions={1} | all-to-all | bytes 2097152 | tf_op jit(solution)/shard_map/all_to_all | solution.py:44
  137.6 1.1 copy.29
  138.7 5.0 %all-to-all-start.2 = ((bf16[32,2,2,8,512]{4,3,2,1,0:T(8,128)(2,1)}), bf16[32,2,2,8,512]{4,3,2,1,0:T(8,128)(2,1)S(1)}, u32[]{:S(2)}, u32[]{:S(2)}) async-start(bf16[32,2,2,8,512]{4,3,2,1,0:T(8,128)(2,1)} %copy.29), calls=%async_computation.2 | async-start | bytes 2097152 | tf_op jit(solution)/shard_map/all_to_all | solution.py:44
  143.7 28.4 %all-to-all-done.2 = bf16[32,2,2,8,512]{4,3,2,1,0:T(8,128)(2,1)S(1)} async-done(((bf16[32,2,2,8,512]{4,3,2,1,0:T(8,128)(2,1)}), bf16[32,2,2,8,512]{4,3,2,1,0:T(8,128)(2,1)S(1)}, u32[]{:S(2)}, u32[]{:S(2)}) %all-to-all-start.2) | async-done | bytes 1048608 | tf_op jit(solution)/shard_map/all_to_all | solution.py:44
  172.1 1.7 bitcast_convert_fusion
  173.8 1.6 broadcast_in_dim.43
  175.4 17.6 %scatter_fusion = f32[128,8,512]{2,1,0:T(8,128)} fusion(f32[128,8,512]{2,1,0:T(8,128)} %broadcast_in_dim.43, s32[128]{0:T(128)S(1)} %compare_select_fusion, f32[128,8,512]{2,1,0:T(8,128)} %bitcast_convert_fusion), kind=kCustom, calls=%fused_computation.1 | custom fusion | bytes 6291968 | tf_op jit(solution)/shard_map/scatter | solution.py:91
  193.0 5.8 %convolution_convert_fusion.1 = bf16[2,512,512]{2,1,0:T(8,128)(2,1)S(1)} fusion(bf16[2,512,2048]{2,1,0:T(8,128)(2,1)} %all-gather.2.cloned.1.call-done), kind=kOutput, calls=%fused_computation.13 | convolution fusion | flops 2148007936 | bytes 5242880 | tf_op jit(solution)/shard_map/jfd,jgd->jfg/dot_general | solution.py:82
  198.8 7.3 %add_convert_fusion = bf16[2,512,2048]{2,1,0:T(8,128)(2,1)} fusion(bf16[2,512,2048]{2,1,0:T(8,128)(2,1)} %all-gather.2.cloned.1.call-done, bf16[2,512,512]{2,1,0:T(8,128)(2,1)S(1)} %convolution_convert_fusion.1), kind=kOutput, calls=%fused_computation.2 | convolution fusion | flops 2695364608 | bytes 9437184 | tf_op jit(solution)/shard_map/jfg,jgd->jfd/dot_general | solution.py:61
  206.2 5.8 %convolution_convert_fusion = bf16[2,512,512]{2,1,0:T(8,128)(2,1)S(1)} fusion(bf16[2,512,2048]{2,1,0:T(8,128)(2,1)} %add_convert_fusion), kind=kOutput, calls=%fused_computation.12 | convolution fusion | flops 2148007936 | bytes 5242880 | tf_op jit(solution)/shard_map/jfd,jgd->jfg/dot_general | solution.py:82
  212.0 8.3 %fusion.3 = f32[2,512,2048]{2,1,0:T(8,128)} fusion(bf16[2,512,2048]{2,1,0:T(8,128)(2,1)} %add_convert_fusion, bf16[2,512,512]{2,1,0:T(8,128)(2,1)S(1)} %convolution_convert_fusion), kind=kOutput, calls=%fused_computation.18 | convolution fusion | flops 2686976000 | bytes 13631488 | tf_op jit(solution)/shard_map/jfg,jgd->jfd/dot_general | solution.py:61
  220.3 3.6 %convert_multiply_fusion = f32[2,512,512]{2,1,0:T(8,128)} fusion(f32[2,512,2048]{2,1,0:T(8,128)} %fusion.3, s32[]{:T(128)S(6)} %select_n.20, bf16[2,512,2048]{2,1,0:T(8,128)(2,1)} %add_convert_fusion), kind=kLoop, calls=%fused_computation.6 | loop fusion | flops 3145728 | bytes 5242884 | tf_op jit(solution)/shard_map/mul | solution.py:87
  (52 shorter events, 23.2 us)
Async XLA Ops:
  7.2 1.6 copy-start
  52.2 12.4 %copy-start.1 = (s32[512]{0:T(512)S(1)}, s32[512]{0:T(512)}, u32[]{:S(2)}) copy-start(s32[512]{0:T(512)} %param.8) | copy-start | bytes 6148
  52.2 63.5 %copy-start.2 = (bf16[512,512]{1,0:T(8,128)(2,1)S(1)}, bf16[512,512]{1,0:T(8,128)(2,1)}, u32[]{:S(2)}) copy-start(bf16[512,512]{1,0:T(8,128)(2,1)} %param.6) | copy-start | bytes 1572868
  52.2 63.5 %all-to-all-start = ((f32[64,2,8,512]{3,2,1,0:T(8,128)}), f32[64,2,8,512]{3,2,1,0:T(8,128)}, u32[]{:S(2)}, u32[]{:S(2)}) async-start(f32[64,2,8,512]{3,2,1,0:T(8,128)} %constant_dynamic-update-slice_fusion), calls=%async_computation | async-start | bytes 4194304 | tf_op jit(solution)/shard_map/all_to_all | solution.py:70
  64.6 128.5 %all-gather.2.cloned.1.call-start = ((), (), s32[]{:S(2)}) async-start(), calls=%async_computation.4 | async-start | bytes 5242880 | tf_op jit(solution)/shard_map/all_gather | solution.py:80
  138.7 33.4 %all-to-all-start.2 = ((bf16[32,2,2,8,512]{4,3,2,1,0:T(8,128)(2,1)}), bf16[32,2,2,8,512]{4,3,2,1,0:T(8,128)(2,1)S(1)}, u32[]{:S(2)}, u32[]{:S(2)}) async-start(bf16[32,2,2,8,512]{4,3,2,1,0:T(8,128)(2,1)} %copy.29), calls=%async_computation.2 | async-start | bytes 2097152 | tf_op jit(solution)/shard_map/all_to_all | solution.py:44
Sparse Core Ops, SparseCore 0:
  133.0 45.1 all-gather.1
